TPU v7x, 512 devices: a whole 4x4x16 slice. The times are simulated.
512 devices in a mesh: blk: 32 (over y, x, core), mpo: 16 (over z).
Axes of the slice: x: 4, y: 4, z: 16, core: 2. Of those that a mesh axis runs over, the one named last changes fastest.
Arguments:
- theta: float32 [64, 128, 16, 128], P('blk'), may hold values from -6 to 6
- block_dims: int32 [64, 2], P('blk'), may hold values from 32 to 128, as said below
- pair_mask: int32 [96, 64], P(None, 'blk'), may hold values 0 or 1
- term_charge: int32 [96], replicated, may hold values from -1 to 1
- left_env: float32 [96, 64, 128, 128], P('mpo', 'blk'), may hold values from -0.5 to 0.5
- right_env: float32 [96, 64, 128, 128], P('mpo', 'blk'), may hold values from -0.5 to 0.5
- site_one: float32 [96, 4, 4], replicated, may hold values from -0.3125 to 0.3125
- site_two: float32 [96, 4, 4], replicated, may hold values from -3 to 3
Outputs:
- hpsi: float32 [64, 128, 16, 128], P('blk', 'mpo')
Inputs may be any that keep to these rules, and one draw needn't show every extreme that they name: `block_dims`: kept dimensions of each sector; rows and columns of a block beyond them are empty. The first sector keeps 128 on both sides.
All inputs are finite; a program needn't handle non-finite values. No bound on the sum of `pair_mask` on one device may be relied on, other than what follows from the above.
Results may differ from a plain program's by a relative error of at most 0.0003.
Values sent between devices are 32-bit elements; how exact they have to be, the bound alone decides.
A program may use at most 64 MiB of HBM per device.

v0:
```python
import jax
import jax.numpy as jnp
from jax import lax
from jax.sharding import PartitionSpec as P


def extended(cells, sides, width):
    for axis, dim in sides:
        count = lax.axis_size(axis)
        ends = count - 1
        head = lax.slice_in_dim(cells, 0, width, axis=dim)
        tail = lax.slice_in_dim(cells, cells.shape[dim] - width, cells.shape[dim], axis=dim)
        cells = jnp.concatenate(
            [
                lax.ppermute(tail, axis, [(i, (i + 1) % count) for i in range(ends)]),
                cells,
                lax.ppermute(head, axis, [((i + 1) % count, i) for i in range(ends)]),
            ],
            axis=dim,
        )
    return cells


def sector_mask(block_dims, bond_cap):
    positions = jnp.arange(bond_cap, dtype=jnp.int32)
    left_ok = positions[None, :] < block_dims[:, 0:1]
    right_ok = positions[None, :] < block_dims[:, 1:2]
    return (left_ok[:, :, None] & right_ok[:, None, :]).astype(jnp.float32)


def make_pair(first_op, second_op):
    states = first_op.shape[0]
    return (first_op[:, None, :, None] * second_op[None, :, None, :]).reshape(
        states * states, states * states
    )


def apply_term(left_rows, source, site_pair, right_block):
    highest = lax.Precision.HIGHEST
    row_count = left_rows.shape[0]
    moved = jnp.dot(
        left_rows,
        source.reshape(source.shape[0], -1),
        precision=highest,
        preferred_element_type=jnp.float32,
    )
    moved = moved.reshape(row_count, source.shape[1], source.shape[2])
    mixed = jnp.einsum("pq,aqd->apd", site_pair, moved, precision=highest)
    return jnp.einsum("apd,bd->apb", mixed, right_block, precision=highest)


def all_sectors(running, padded, left_all, right_all, charge, site_pair, allowed):
    sectors = left_all.shape[0]
    source_index = jnp.arange(sectors, dtype=jnp.int32) + 1 - charge

    def per_sector(left_rows, index, right_block):
        source = lax.dynamic_index_in_dim(padded, index, 0, keepdims=False)
        return apply_term(left_rows, source, site_pair, right_block)

    terms = jax.vmap(per_sector)(left_all, source_index, right_all)
    return running + allowed.astype(jnp.float32)[:, None, None, None] * terms


def body(theta, block_dims, pair_mask, term_charge, left_env, right_env, site_one, site_two):
    bond_cap = theta.shape[1]
    group_index = lax.axis_index("mpo")
    group_count = lax.axis_size("mpo")
    row_count = bond_cap // group_count
    first_row = group_index * row_count
    block_mask = sector_mask(block_dims, bond_cap)
    masked = theta * block_mask[:, :, None, :]
    padded = extended(masked, (("blk", 0),), 1)
    row_mask = lax.dynamic_slice_in_dim(block_mask, first_row, row_count, 1)
    term_count = left_env.shape[0]
    first_term = group_index * term_count

    def local_term(w, running):
        term_index = first_term + w
        charge = lax.dynamic_index_in_dim(term_charge, term_index, 0, keepdims=False)
        allowed = lax.dynamic_index_in_dim(pair_mask, term_index, 0, keepdims=False)
        first_op = lax.dynamic_index_in_dim(site_one, term_index, 0, keepdims=False)
        second_op = lax.dynamic_index_in_dim(site_two, term_index, 0, keepdims=False)
        left_all = lax.dynamic_index_in_dim(left_env, w, 0, keepdims=False)
        right_all = lax.dynamic_index_in_dim(right_env, w, 0, keepdims=False)
        return all_sectors(
            running, padded, left_all, right_all, charge, make_pair(first_op, second_op), allowed
        )

    partial_value = lax.fori_loop(0, term_count, local_term, jnp.zeros(theta.shape, jnp.float32))
    whole_sum = lax.psum(partial_value, "mpo")
    mine = lax.dynamic_slice_in_dim(whole_sum, first_row, row_count, 1)
    return mine * row_mask[:, :, None, :]


def solution(mesh):
    placed = (
        P("blk", None, None, None),
        P("blk", None),
        P(None, "blk"),
        P(),
        P("mpo", "blk", None, None),
        P("mpo", "blk", None, None),
        P(),
        P(),
    )
    return jax.shard_map(
        body, mesh=mesh, in_specs=placed, out_specs=P("blk", "mpo", None, None), check_vma=False
    )
```

profile of v0, /device:TPU:2, one launch (start us, length us, event | category | flops | bytes accessed | tf_op | source)
XLA Modules:
  0.0 307.2 jit_solution(4016067030616916532)
XLA Ops:
  7.7 2.2 copy_multiply_fusion
  11.1 1.9 collective-permute-start
  13.1 3.6 %collective-permute-start.1 = (f32[1,128,16,128]{3,1,2,0:T(8,128)S(1)}, f32[1,128,16,128]{3,1,2,0:T(8,128)}, u32[]{:S(2)}, u32[]{:S(2)}) collective-permute-start(f32[1,128,16,128]{3,1,2,0:T(8,128)S(1)} %get-tuple-element.253), channel_id=1, source_target_pairs={{16,0},{32,16},{48,32},{64,48},{80,64},{96,80},{112,96},{128,112},... | collective-permute-start | bytes 3145736 | tf_op jit(solution)/shard_map/ppermute | solution.py:17
  17.8 9.7 %collective-permute-done = f32[1,128,16,128]{3,1,2,0:T(8,128)} collective-permute-done((f32[1,128,16,128]{3,1,2,0:T(8,128)}, f32[1,128,16,128]{3,1,2,0:T(8,128)}, u32[]{:S(2)}, u32[]{:S(2)}) %collective-permute-start) | collective-permute-done | bytes 1048608 | tf_op jit(solution)/shard_map/ppermute | solution.py:15
  29.0 4.0 %pad_maximum_fusion = f32[4,128,16,128]{3,1,2,0:T(8,128)} fusion(f32[1,128,16,128]{3,1,2,0:T(8,128)} %collective-permute-done.1, f32[2,128,16,128]{3,1,2,0:T(8,128)S(1)} %copy_multiply_fusion, f32[1,128,16,128]{3,1,2,0:T(8,128)} %collective-permute-done), kind=kLoop, calls=%fused_computation.25 | loop fusion | flops 2097152 | bytes 8388608 | tf_op jit(solution)/shard_map/concatenate | solution.py:13
  33.0 109.8 %while.14 = (s32[]{:T(128)}, f32[2,128,16,128]{3,1,2,0:T(8,128)}, s32[]{:T(128)}, s32[96,2]{1,0:T(8,128)S(1)}, f32[6,2,128,128]{3,2,1,0:T(8,128)}, /*index=5*/s3...) while((s32[]{:T(128)}, f32[2,128,16,128]{3,1,2,0:T(8,128)}, ...), condition=%wide.region_1.2_spmd.clone, body=%wide.region_0.1_spmd.clone.sunk | while | flops 1712849152 | bytes 44307156 | solution.py:89
  35.0 2.9 gather_fusion
  39.7 3.6 %fusion.37 = f32[2,128,2048]{2,1,0:T(8,128)S(1)} fusion(f32[2,128,2048]{1,2,0:T(8,128)} %bitcast.61, f32[6,2,128,128]{3,2,1,0:T(8,128)} %get-tuple-element.351, s32[]{:T(128)S(6)} %copy.41), kind=kOutput, calls=%fused_computation.8.clone.1 | convolution fusion | flops 805306368 | bytes 4325380 | tf_op jit(solution)/shard_map/while/body/eval_jaxpr/vmap()/dot_general | solution.py:41
  43.7 1.9 fusion.38
  45.6 4.4 %select_add_fusion.2 = f32[2,128,16,128]{3,1,2,0:T(8,128)S(1)} fusion(f32[2,128,16,128]{3,1,2,0:T(8,128)S(1)} %copy-done, f32[2,128,128,16]{2,3,1,0:T(8,128)S(1)} %fusion.38, f32[2]{0:T(128)S(1)} %fusion.39, pred[]{:T(512)S(6)} %compare.3, f32[6,2,128,128]{3,2,1,0:T(8,128)} %get-tuple-element.356, s32[]{:T(128)S(6)} %copy.41), kind=kOutput, calls=%fused_computation.6.clone.1 | convolution fusion | flops 806879232 | bytes 6422541 | tf_op jit(solution)/shard_map/while/body/eval_jaxpr/vmap(apd,bd->apb)/dot_general | solution.py:49
  53.3 2.9 gather_fusion
  58.0 3.6 %fusion.37 = f32[2,128,2048]{2,1,0:T(8,128)S(1)} fusion(f32[2,128,2048]{1,2,0:T(8,128)} %bitcast.61, f32[6,2,128,128]{3,2,1,0:T(8,128)} %get-tuple-element.351, s32[]{:T(128)S(6)} %copy.41), kind=kOutput, calls=%fused_computation.8.clone.1 | convolution fusion | flops 805306368 | bytes 4325380 | tf_op jit(solution)/shard_map/while/body/eval_jaxpr/vmap()/dot_general | solution.py:41
  62.0 1.9 fusion.38
  63.9 4.4 %select_add_fusion.2 = f32[2,128,16,128]{3,1,2,0:T(8,128)S(1)} fusion(f32[2,128,16,128]{3,1,2,0:T(8,128)S(1)} %copy-done, f32[2,128,128,16]{2,3,1,0:T(8,128)S(1)} %fusion.38, f32[2]{0:T(128)S(1)} %fusion.39, pred[]{:T(512)S(6)} %compare.3, f32[6,2,128,128]{3,2,1,0:T(8,128)} %get-tuple-element.356, s32[]{:T(128)S(6)} %copy.41), kind=kOutput, calls=%fused_computation.6.clone.1 | convolution fusion | flops 806879232 | bytes 6422541 | tf_op jit(solution)/shard_map/while/body/eval_jaxpr/vmap(apd,bd->apb)/dot_general | solution.py:49
  71.6 2.9 gather_fusion
  76.3 3.6 %fusion.37 = f32[2,128,2048]{2,1,0:T(8,128)S(1)} fusion(f32[2,128,2048]{1,2,0:T(8,128)} %bitcast.61, f32[6,2,128,128]{3,2,1,0:T(8,128)} %get-tuple-element.351, s32[]{:T(128)S(6)} %copy.41), kind=kOutput, calls=%fused_computation.8.clone.1 | convolution fusion | flops 805306368 | bytes 4325380 | tf_op jit(solution)/shard_map/while/body/eval_jaxpr/vmap()/dot_general | solution.py:41
  80.3 1.9 fusion.38
  82.2 4.4 %select_add_fusion.2 = f32[2,128,16,128]{3,1,2,0:T(8,128)S(1)} fusion(f32[2,128,16,128]{3,1,2,0:T(8,128)S(1)} %copy-done, f32[2,128,128,16]{2,3,1,0:T(8,128)S(1)} %fusion.38, f32[2]{0:T(128)S(1)} %fusion.39, pred[]{:T(512)S(6)} %compare.3, f32[6,2,128,128]{3,2,1,0:T(8,128)} %get-tuple-element.356, s32[]{:T(128)S(6)} %copy.41), kind=kOutput, calls=%fused_computation.6.clone.1 | convolution fusion | flops 806879232 | bytes 6422541 | tf_op jit(solution)/shard_map/while/body/eval_jaxpr/vmap(apd,bd->apb)/dot_general | solution.py:49
  89.9 2.9 gather_fusion
  94.6 3.6 %fusion.37 = f32[2,128,2048]{2,1,0:T(8,128)S(1)} fusion(f32[2,128,2048]{1,2,0:T(8,128)} %bitcast.61, f32[6,2,128,128]{3,2,1,0:T(8,128)} %get-tuple-element.351, s32[]{:T(128)S(6)} %copy.41), kind=kOutput, calls=%fused_computation.8.clone.1 | convolution fusion | flops 805306368 | bytes 4325380 | tf_op jit(solution)/shard_map/while/body/eval_jaxpr/vmap()/dot_general | solution.py:41
  98.6 1.9 fusion.38
  100.5 4.4 %select_add_fusion.2 = f32[2,128,16,128]{3,1,2,0:T(8,128)S(1)} fusion(f32[2,128,16,128]{3,1,2,0:T(8,128)S(1)} %copy-done, f32[2,128,128,16]{2,3,1,0:T(8,128)S(1)} %fusion.38, f32[2]{0:T(128)S(1)} %fusion.39, pred[]{:T(512)S(6)} %compare.3, f32[6,2,128,128]{3,2,1,0:T(8,128)} %get-tuple-element.356, s32[]{:T(128)S(6)} %copy.41), kind=kOutput, calls=%fused_computation.6.clone.1 | convolution fusion | flops 806879232 | bytes 6422541 | tf_op jit(solution)/shard_map/while/body/eval_jaxpr/vmap(apd,bd->apb)/dot_general | solution.py:49
  108.2 2.9 gather_fusion
  112.9 3.6 %fusion.37 = f32[2,128,2048]{2,1,0:T(8,128)S(1)} fusion(f32[2,128,2048]{1,2,0:T(8,128)} %bitcast.61, f32[6,2,128,128]{3,2,1,0:T(8,128)} %get-tuple-element.351, s32[]{:T(128)S(6)} %copy.41), kind=kOutput, calls=%fused_computation.8.clone.1 | convolution fusion | flops 805306368 | bytes 4325380 | tf_op jit(solution)/shard_map/while/body/eval_jaxpr/vmap()/dot_general | solution.py:41
  116.9 1.9 fusion.38
  118.8 4.4 %select_add_fusion.2 = f32[2,128,16,128]{3,1,2,0:T(8,128)S(1)} fusion(f32[2,128,16,128]{3,1,2,0:T(8,128)S(1)} %copy-done, f32[2,128,128,16]{2,3,1,0:T(8,128)S(1)} %fusion.38, f32[2]{0:T(128)S(1)} %fusion.39, pred[]{:T(512)S(6)} %compare.3, f32[6,2,128,128]{3,2,1,0:T(8,128)} %get-tuple-element.356, s32[]{:T(128)S(6)} %copy.41), kind=kOutput, calls=%fused_computation.6.clone.1 | convolution fusion | flops 806879232 | bytes 6422541 | tf_op jit(solution)/shard_map/while/body/eval_jaxpr/vmap(apd,bd->apb)/dot_general | solution.py:49
  126.5 2.9 gather_fusion
  131.2 3.6 %fusion.37 = f32[2,128,2048]{2,1,0:T(8,128)S(1)} fusion(f32[2,128,2048]{1,2,0:T(8,128)} %bitcast.61, f32[6,2,128,128]{3,2,1,0:T(8,128)} %get-tuple-element.351, s32[]{:T(128)S(6)} %copy.41), kind=kOutput, calls=%fused_computation.8.clone.1 | convolution fusion | flops 805306368 | bytes 4325380 | tf_op jit(solution)/shard_map/while/body/eval_jaxpr/vmap()/dot_general | solution.py:41
  135.2 1.9 fusion.38
  137.1 4.4 %select_add_fusion.2 = f32[2,128,16,128]{3,1,2,0:T(8,128)S(1)} fusion(f32[2,128,16,128]{3,1,2,0:T(8,128)S(1)} %copy-done, f32[2,128,128,16]{2,3,1,0:T(8,128)S(1)} %fusion.38, f32[2]{0:T(128)S(1)} %fusion.39, pred[]{:T(512)S(6)} %compare.3, f32[6,2,128,128]{3,2,1,0:T(8,128)} %get-tuple-element.356, s32[]{:T(128)S(6)} %copy.41), kind=kOutput, calls=%fused_computation.6.clone.1 | convolution fusion | flops 806879232 | bytes 6422541 | tf_op jit(solution)/shard_map/while/body/eval_jaxpr/vmap(apd,bd->apb)/dot_general | solution.py:49
  142.8 4.2 %copy.20 = f32[2,128,16,128]{3,2,1,0:T(8,128)} copy(f32[2,128,16,128]{3,1,2,0:T(8,128)} %get-tuple-element.174) | data formatting | bytes 4194304 | tf_op jit(solution)/shard_map/while | solution.py:89
  147.0 151.8 %all-reduce.2.cloned.1.call-done = f32[2,128,16,128]{3,2,1,0:T(8,128)} async-done(((f32[2,128,16,128]{3,2,1,0:T(8,128)}), f32[2,128,16,128]{3,2,1,0:T(8,128)}) %all-reduce.2.cloned.1.call-update) | async-done | bytes 2097168 | tf_op jit(solution)/shard_map/psum | solution.py:90
  (93 shorter events, 39.6 us)
Async XLA Ops:
  6.5 292.3 %all-reduce.2.cloned.1.call-start = ((), (), s32[]{:S(2)}) async-start(), calls=%async_computation | async-start | bytes 4194304 | tf_op jit(solution)/shard_map/psum | solution.py:90
  9.9 6.8 %copy-start.4 = (s32[96,2]{0,1:T(2,128)S(1)}, s32[96,2]{0,1:T(2,128)}, u32[]{:S(2)}) copy-start(s32[96,2]{0,1:T(2,128)} %param.12) | copy-start | bytes 2308
  10.0 6.9 %copy-start.2 = (f32[96,4,4]{0,2,1:T(4,128)S(1)}, f32[96,4,4]{0,2,1:T(4,128)}, u32[]{:S(2)}) copy-start(f32[96,4,4]{0,2,1:T(4,128)} %param.16) | copy-start | bytes 18436
  10.0 7.0 %copy-start.3 = (f32[96,4,4]{0,2,1:T(4,128)S(1)}, f32[96,4,4]{0,2,1:T(4,128)}, u32[]{:S(2)}) copy-start(f32[96,4,4]{0,2,1:T(4,128)} %param.17) | copy-start | bytes 18436
  11.1 16.4 %collective-permute-start = (f32[1,128,16,128]{3,1,2,0:T(8,128)}, f32[1,128,16,128]{3,1,2,0:T(8,128)}, u32[]{:S(2)}, u32[]{:S(2)}) collective-permute-start(f32[1,128,16,128]{3,1,2,0:T(8,128)} %get-tuple-element.252), channel_id=1, source_target_pairs={{0,16},{16,32},{32,48},{48,64},{64,80},{80,96},{96,112},{112,128},... | collective-permute-start | bytes 3145736 | tf_op jit(solution)/shard_map/ppermute | solution.py:15
  13.1 15.9 %collective-permute-start.1 = (f32[1,128,16,128]{3,1,2,0:T(8,128)S(1)}, f32[1,128,16,128]{3,1,2,0:T(8,128)}, u32[]{:S(2)}, u32[]{:S(2)}) collective-permute-start(f32[1,128,16,128]{3,1,2,0:T(8,128)S(1)} %get-tuple-element.253), channel_id=1, source_target_pairs={{16,0},{32,16},{48,32},{64,48},{80,64},{96,80},{112,96},{128,112},... | collective-permute-start | bytes 3145736 | tf_op jit(solution)/shard_map/ppermute | solution.py:17
  17.8 15.1 %copy-start.5 = (s32[96]{0:T(128)S(1)}, s32[96]{0:T(128)}, u32[]{:S(2)}) copy-start(s32[96]{0:T(128)} %param.13) | copy-start | bytes 1156
  43.7 1.9 copy-start
  49.9 1.3 copy-start.1
  62.0 1.9 copy-start
  68.3 1.3 copy-start.1
  80.3 1.9 copy-start
  86.6 1.3 copy-start.1
  98.6 1.9 copy-start
  104.9 1.3 copy-start.1
  116.9 1.9 copy-start
  123.2 1.3 copy-start.1
  135.2 1.9 copy-start
  141.5 1.3 copy-start.1
Sparse Core Ops, SparseCore 0:
  147.1 151.6 all-reduce.1
where the time goes:
time: 308 us; the launch traced here: 307 us
  waiting for transfers between devices  163 us (53%)
  matrix products  58.9 us (19%)
  local copies, waits for them, and re-layouts  53.9 us (18%)
  between operations  13.5 us (4%)
  other arithmetic  11.8 us (4%)
  starting transfers between devices  5.55 us (2%)
    psum x1, waiting for transfers between devices, body(): whole_sum = lax.psum(partial_value, 'mpo')  152 us
    gather x12, local copies, waits for them, and re-layouts, per_sector(): source = lax.dynamic_index_in_dim(padded, index, 0, keepdims=False)  28.4 us
    dot_general x6, matrix products, apply_term(): return jnp.einsum('apd,bd->apb', mixed, right_block, precision=highest)  26.2 us
    dot_general x6, matrix products, apply_term(): jnp.dot(left_rows, source.reshape(source.shape[0], -1), precision=highest...  21.4 us
    dot_general x6, matrix products, apply_term(): mixed = jnp.einsum('pq,aqd->apd', site_pair, moved, precision=highest)  11.3 us
    while x30, local copies, waits for them, and re-layouts  10.3 us
    ppermute x1, waiting for transfers between devices, extended(): lax.ppermute(tail, axis, [(i, (i + 1) % count) for i in range(ends)])  9.72 us
  transfers between devices with their start and end apart: 3, of which 3 were waited for; matrix products, arithmetic and copies ran while one was open for 0% of the time, Pallas kernels for 0%

commit v1 on v0

--- a/solution.py
+++ b/solution.py
@@ -87,7 +87,7 @@
         )
 
     partial_value = lax.fori_loop(0, term_count, local_term, jnp.zeros(theta.shape, jnp.float32))
-    whole_sum = lax.psum(partial_value, "mpo")
+    whole_sum = jnp.sum(lax.all_gather(partial_value, "mpo"), axis=0)
     mine = lax.dynamic_slice_in_dim(whole_sum, first_row, row_count, 1)
     return mine * row_mask[:, :, None, :]
 

time: 308 us -> 535 us (1.74)
  the two profiles are of different devices: /device:TPU:2 before, /device:TPU:1 now
where the time goes in v1:
time: 535 us; the launch traced here: 534 us
  waiting for transfers between devices  373 us (70%)
  matrix products  59.1 us (11%)
  local copies, waits for them, and re-layouts  54.6 us (10%)
  other arithmetic  22.3 us (4%)
  between operations  13.5 us (3%)
  starting transfers between devices  11 us (2%)
    all_gather x1, waiting for transfers between devices, body(): whole_sum = jnp.sum(lax.all_gather(partial_value, 'mpo'), axis=0)  364 us
    gather x12, local copies, waits for them, and re-layouts, per_sector(): source = lax.dynamic_index_in_dim(padded, index, 0, keepdims=False)  28.4 us
    dot_general x6, matrix products, apply_term(): return jnp.einsum('apd,bd->apb', mixed, right_block, precision=highest)  26.2 us
    dot_general x6, matrix products, apply_term(): jnp.dot(left_rows, source.reshape(source.shape[0], -1), precision=highest...  21.4 us
    reduce_sum x1, other arithmetic, body(): whole_sum = jnp.sum(lax.all_gather(partial_value, 'mpo'), axis=0)  12.1 us
    dot_general x6, matrix products, apply_term(): mixed = jnp.einsum('pq,aqd->apd', site_pair, moved, precision=highest)  11.5 us
  transfers between devices with their start and end apart: 3, of which 3 were waited for; matrix products, arithmetic and copies ran while one was open for 0% of the time, Pallas kernels for 0%

profile of v1, /device:TPU:1, one launch (start us, length us, event | category | flops | bytes accessed | tf_op | source)
XLA Modules:
  0.0 533.7 jit_solution(6946920197046462683)
XLA Ops:
  7.7 2.2 copy_multiply_fusion
  11.1 4.5 collective-permute-start
  15.6 6.5 %collective-permute-start.1 = (f32[1,128,16,128]{3,1,2,0:T(8,128)S(1)}, f32[1,128,16,128]{3,1,2,0:T(8,128)}, u32[]{:S(2)}, u32[]{:S(2)}) collective-permute-start(f32[1,128,16,128]{3,1,2,0:T(8,128)S(1)} %get-tuple-element.263), channel_id=1, source_target_pairs={{16,0},{32,16},{48,32},{64,48},{80,64},{96,80},{112,96},{128,112},... | collective-permute-start | bytes 3145736 | tf_op jit(solution)/shard_map/ppermute | solution.py:17
  23.3 4.4 collective-permute-done
  27.7 4.2 collective-permute-done.1
  31.9 3.9 pad_maximum_fusion
  35.7 110.0 %while.14 = (s32[]{:T(128)}, f32[2,128,16,128]{3,1,2,0:T(8,128)}, s32[]{:T(128)}, s32[96,2]{1,0:T(8,128)S(1)}, f32[6,2,128,128]{3,2,1,0:T(8,128)}, /*index=5*/s3...) while((s32[]{:T(128)}, f32[2,128,16,128]{3,1,2,0:T(8,128)}, ...), condition=%wide.region_1.2_spmd.clone, body=%wide.region_0.1_spmd.clone.sunk | while | flops 1712849152 | bytes 44307156 | solution.py:89
  37.7 2.9 gather_fusion
  42.4 3.6 fusion.39
  48.3 4.4 select_add_fusion.2
  56.0 2.9 gather_fusion
  60.8 3.6 fusion.39
  64.7 1.9 fusion.40
  66.7 4.4 select_add_fusion.2
  74.4 2.9 gather_fusion
  79.1 3.6 fusion.39
  85.0 4.4 select_add_fusion.2
  92.7 2.9 gather_fusion
  97.4 3.6 fusion.39
  101.4 1.9 fusion.40
  103.4 4.4 select_add_fusion.2
  111.0 2.9 gather_fusion
  115.8 3.6 fusion.39
  119.8 1.9 fusion.40
  121.7 4.4 select_add_fusion.2
  129.4 2.9 gather_fusion
  134.1 3.6 fusion.39
  138.1 1.9 fusion.40
  140.0 4.4 select_add_fusion.2
  145.7 4.1 copy.26
  149.9 364.0 %all-gather.3.cloned.1.call-done = f32[32,128,16,128]{3,2,1,0:T(8,128)} async-done(((f32[2,128,16,128]{3,2,1,0:T(8,128)}), f32[32,128,16,128]{3,2,1,0:T(8,128)}) %all-gather.3.cloned.1.call-update) | async-done | bytes 33554448 | tf_op jit(solution)/shard_map/all_gather | solution.py:90
  514.0 12.1 %reduce_sum.9 = f32[2,128,16,128]{3,2,1,0:T(8,128)S(1)} reduce(f32[16,2,128,16,128]{4,3,2,1,0:T(8,128)} %bitcast.63, f32[]{:T(128)} %constant.69.clone.1), dimensions={0}, to_apply=%region_2.3 | reduce | flops 7864320 | bytes 35651588 | tf_op jit(solution)/shard_map/reduce_sum | solution.py:90
  (96 shorter events, 41.2 us)
Async XLA Ops:
  6.5 507.4 %all-gather.3.cloned.1.call-start = ((), (), s32[]{:S(2)}) async-start(), calls=%async_computation | async-start | bytes 35651584 | tf_op jit(solution)/shard_map/all_gather | solution.py:90
  9.9 12.2 %copy-start.4 = (s32[96,2]{0,1:T(2,128)S(1)}, s32[96,2]{0,1:T(2,128)}, u32[]{:S(2)}) copy-start(s32[96,2]{0,1:T(2,128)} %param.12) | copy-start | bytes 2308
  10.0 12.3 %copy-start.2 = (f32[96,4,4]{0,2,1:T(4,128)S(1)}, f32[96,4,4]{0,2,1:T(4,128)}, u32[]{:S(2)}) copy-start(f32[96,4,4]{0,2,1:T(4,128)} %param.16) | copy-start | bytes 18436
  10.0 12.5 %copy-start.3 = (f32[96,4,4]{0,2,1:T(4,128)S(1)}, f32[96,4,4]{0,2,1:T(4,128)}, u32[]{:S(2)}) copy-start(f32[96,4,4]{0,2,1:T(4,128)} %param.17) | copy-start | bytes 18436
  11.1 16.5 %collective-permute-start = (f32[1,128,16,128]{3,1,2,0:T(8,128)}, f32[1,128,16,128]{3,1,2,0:T(8,128)}, u32[]{:S(2)}, u32[]{:S(2)}) collective-permute-start(f32[1,128,16,128]{3,1,2,0:T(8,128)} %get-tuple-element.262), channel_id=1, source_target_pairs={{0,16},{16,32},{32,48},{48,64},{64,80},{80,96},{96,112},{112,128},... | collective-permute-start | bytes 3145736 | tf_op jit(solution)/shard_map/ppermute | solution.py:15
  15.6 16.2 %collective-permute-start.1 = (f32[1,128,16,128]{3,1,2,0:T(8,128)S(1)}, f32[1,128,16,128]{3,1,2,0:T(8,128)}, u32[]{:S(2)}, u32[]{:S(2)}) collective-permute-start(f32[1,128,16,128]{3,1,2,0:T(8,128)S(1)} %get-tuple-element.263), channel_id=1, source_target_pairs={{16,0},{32,16},{48,32},{64,48},{80,64},{96,80},{112,96},{128,112},... | collective-permute-start | bytes 3145736 | tf_op jit(solution)/shard_map/ppermute | solution.py:17
  23.3 12.4 %copy-start.5 = (s32[96]{0:T(128)S(1)}, s32[96]{0:T(128)}, u32[]{:S(2)}) copy-start(s32[96]{0:T(128)} %param.13) | copy-start | bytes 1156
  46.4 1.9 copy-start
  52.7 1.3 copy-start.1
  64.7 1.9 copy-start
  71.1 1.3 copy-start.1
  83.1 1.9 copy-start
  89.4 1.3 copy-start.1
  101.4 1.9 copy-start
  107.7 1.3 copy-start.1
  119.8 1.9 copy-start
  126.1 1.3 copy-start.1
  138.1 1.9 copy-start
  144.4 1.3 copy-start.1
Sparse Core Ops, SparseCore 0:
  150.0 363.8 all-gather.2
